TPU v7x, 32 devices: a whole 2x2x4 slice. The times are simulated.
32 devices in a mesh: dp: 4 (over x, core), fsdp: 8 (over z, y).
Axes of the slice: x: 2, y: 2, z: 4, core: 2. Of those that a mesh axis runs over, the one named last changes fastest.
Arguments:
- mel_clips: bfloat16 [640, 256, 512], P(('dp', 'fsdp')), may hold values from -6 to 6
- live_counts: int32 [32, 4], P(('dp', 'fsdp')), may hold values from 1 to 5, as said below
- conv_weight: bfloat16 [512, 7], P(('dp', 'fsdp')), may hold values from -2 to 2
- conv_bias: bfloat16 [512], P(('dp', 'fsdp')), may hold values from -3 to 3
- norm_gain: bfloat16 [512], P(('dp', 'fsdp')), may hold values from 0.25 to 1.75
- norm_shift: bfloat16 [512], P(('dp', 'fsdp')), may hold values from -2 to 2
- in_weight: bfloat16 [512, 1536], P(('dp', 'fsdp')), may hold values from -0.25 to 0.25
- in_bias: bfloat16 [1536], P(('dp', 'fsdp')), may hold values from -2 to 2
- out_weight: bfloat16 [1536, 512], P(('dp', 'fsdp')), may hold values from -0.3125 to 0.3125
- out_bias: bfloat16 [512], P(('dp', 'fsdp')), may hold values from -2 to 2
- layer_scale: bfloat16 [512], P(('dp', 'fsdp')), may hold values from 0.29882812 to 1.1953125
- cotangent: bfloat16 [640, 256, 512], P(('dp', 'fsdp')), may hold values from -6 to 6
Outputs:
- block_out: bfloat16 [640, 256, 512], P(('dp', 'fsdp'))
- grad_clips: bfloat16 [640, 256, 512], P(('dp', 'fsdp'))
- grad_conv_weight: float32 [512, 7], P(('dp', 'fsdp'))
- grad_conv_bias: float32 [512], P(('dp', 'fsdp'))
- grad_norm_gain: float32 [512], P(('dp', 'fsdp'))
- grad_norm_shift: float32 [512], P(('dp', 'fsdp'))
- grad_in_weight: float32 [512, 1536], P(('dp', 'fsdp'))
- grad_in_bias: float32 [1536], P(('dp', 'fsdp'))
- grad_out_weight: float32 [1536, 512], P(('dp', 'fsdp'))
- grad_out_bias: float32 [512], P(('dp', 'fsdp'))
- grad_layer_scale: float32 [512], P(('dp', 'fsdp'))
Inputs may be any that keep to these rules, and one draw needn't show every extreme that they name: Slot s of micro-batch m on device d holds a live clip when s < live_counts[d, m]; some device has all 5 slots live in some micro-batch, and some device only one.
All inputs are finite; a program needn't handle non-finite values.
Results may differ from a plain program's by a relative error of at most 0.0063.
Values may be sent and summed in bfloat16 or wider, within the bound.
A program may use at most 256 MiB of HBM per device.

v0:
```python
from functools import partial
import jax
import jax.numpy as jnp
from jax import lax
from jax.experimental import pallas as pl
from jax.experimental.pallas import tpu as pltpu
from jax.sharding import PartitionSpec as P

F32 = jnp.float32
BF16 = jnp.bfloat16
PAD = 8
ROOT_HALF = 0.7071067811865476
LOG2E = 1.4426950408889634
INV_ROOT_2PI = 0.3989422804014327


def dot_nn(a, b):
    return lax.dot_general(a, b, (((1,), (0,)), ((), ())), preferred_element_type=F32)


def dot_nt(a, b):
    return lax.dot_general(a, b, (((1,), (1,)), ((), ())), preferred_element_type=F32)


def fold8(v):
    total = v[0:8]
    for r in range(8, v.shape[0], 8):
        total = total + v[r : r + 8]
    return total


def clip_of(i, counts, slots):
    micros = counts.shape[0]
    lives = [counts[m] for m in range(micros)]
    count = lives[0]
    for m in range(1, micros):
        count = count + lives[m]
    alive = i < count
    rest = jnp.where(alive, i, i - count)
    clip = jnp.int32(0)
    start = jnp.int32(0)
    for m in range(micros):
        length = jnp.where(alive, lives[m], slots - lives[m])
        inside = jnp.logical_and(rest >= start, rest < start + length)
        first = m * slots + jnp.where(alive, 0, lives[m])
        clip = jnp.where(inside, first + rest - start, clip)
        start = start + length
    return clip


def lane_ids(rows):
    return lax.broadcasted_iota(jnp.int32, (rows, 128), 1)


def unpack_small(pieces_ref, kinds, rows_ref, ib_ref):
    devices = pieces_ref.shape[0]
    shard = rows_ref.shape[1] // devices
    wide = ib_ref.shape[1] // devices
    rows_ref[...] = jnp.zeros_like(rows_ref)
    ib_ref[...] = jnp.zeros_like(ib_ref)
    lane = lane_ids(8)
    for d in range(devices):
        piece = pieces_ref[d].astype(F32)
        at, off = divmod(d * shard, 128)
        rows_ref[:, at * 128 : at * 128 + 128] += pltpu.roll(piece, off, 1)
        at, off = divmod(d * wide, 128)
        moved = pltpu.roll(piece[8:16], off, 1)[kinds - 8 : kinds - 7]
        line = lane[0:1]
        ib_ref[0:1, at * 128 : at * 128 + 128] += jnp.where(line >= off, moved, 0.0)
        if off + wide > 128:
            ib_ref[0:1, at * 128 + 128 : at * 128 + 256] += jnp.where(line < off, moved, 0.0)


def pack_small(acc_small, acc_ib, rows_ref, small_ref):
    devices = small_ref.shape[0]
    kinds = acc_small.shape[0]
    shard = rows_ref.shape[1] // devices
    wide = acc_ib.shape[1] // devices
    for k in range(kinds):
        rows_ref[k : k + 1, :] = jnp.sum(acc_small[k], axis=0, keepdims=True)
    lane = lane_ids(16)
    bias = acc_ib[...]
    for d in range(devices):
        at, off = divmod(d * shard, 128)
        moved = pltpu.roll(rows_ref[:, at * 128 : at * 128 + 128], (128 - off) % 128, 1)
        small_ref[d] = jnp.where(lane < shard, moved, 0.0)
        at, off = divmod(d * wide, 128)
        moved = pltpu.roll(bias[:, at * 128 : at * 128 + 128], (128 - off) % 128, 1)
        if off + wide > 128:
            later = pltpu.roll(bias[:, at * 128 + 128 : at * 128 + 256], 128 - off, 1)
            moved = jnp.where(lane[0:8] < 128 - off, moved, later)
        moved = jnp.where(lane[0:8] < wide, moved, 0.0)
        small_ref[d, kinds : kinds + 1, :] = jnp.sum(moved, axis=0, keepdims=True)


def clip_kernel(
    counts_ref,
    x_ref,
    dy_ref,
    xn_ref,
    dyn_ref,
    w_in_ref,
    w_out_ref,
    pieces_ref,
    out_ref,
    gx_ref,
    gin_ref,
    gout_ref,
    small_ref,
    rows_ref,
    ib_ref,
    xp,
    gm,
    xh,
    rs,
    left,
    acts,
    gob,
    nb,
    gn,
    raw,
    acc,
    acc_small,
    acc_ib,
    *,
    taps,
    hid_chunk,
    row_chunk,
    parts,
):
    step = pl.program_id(0)
    _, groups, frames, lanes = xh.shape
    chans = groups * lanes
    hid = acts.shape[2]
    margin = (taps - 1) // 2
    gain, shift, obias, scale = taps + 1, taps + 2, taps + 3, taps + 4
    span = [slice(g * lanes, (g + 1) * lanes) for g in range(groups)]
    now = step % 2
    then = 1 - now
    live_count = counts_ref[0]
    for m in range(1, counts_ref.shape[0]):
        live_count = live_count + counts_ref[m]
    live = step < live_count

    def row(i, g):
        return rows_ref[i : i + 1, span[g]]

    def total(blocks):
        added = blocks[0]
        for block in blocks[1:]:
            added = added + block
        return jnp.sum(added, axis=-1, keepdims=True) * (1.0 / chans)

    def stage(x_in, to):
        for g in range(groups):
            xp[to, g, PAD : PAD + frames, :] = x_in[0, :, span[g]].astype(F32)

    def begin(dy_in, to, start, size):
        for r in range(0, size, row_chunk):
            low = start + r
            at_rows = pl.ds(low, row_chunk)
            mixed = []
            for g in range(groups):
                m = row(taps, g) + xp[to, g, pl.ds(low + (PAD - margin), row_chunk), :] * row(0, g)
                for k in range(1, taps):
                    m = m + xp[to, g, pl.ds(low + (PAD - margin + k), row_chunk), :] * row(k, g)
                mixed.append(m)
            mean = total(mixed)
            center = [m - mean for m in mixed]
            inv = lax.rsqrt(total([c * c for c in center]) + 1e-06)
            rs[to, at_rows, :] = jnp.broadcast_to(inv, (row_chunk, lanes))
            for g in range(groups):
                xhat = center[g] * inv
                xh[to, g, at_rows, :] = xhat
                nb[to, at_rows, span[g]] = (xhat * row(gain, g) + row(shift, g)).astype(BF16)
                gob[to, at_rows, span[g]] = (dy_in[0, at_rows, span[g]].astype(F32) * row(scale, g)).astype(BF16)

    def turn(to):
        left[to, 0] = gob[to].T
        left[to, 1] = nb[to].T

    @pl.when(step == 0)
    def _():
        unpack_small(pieces_ref, taps + 5, rows_ref, ib_ref)
        acc[...] = jnp.zeros_like(acc)
        acc_small[...] = jnp.zeros_like(acc_small)
        acc_ib[...] = jnp.zeros_like(acc_ib)
        edge = jnp.zeros((2, groups, PAD, lanes), F32)
        xp[:, :, 0:PAD, :] = edge
        xp[:, :, PAD + frames :, :] = edge
        gm[:, 0:PAD, :] = edge[0]
        gm[:, PAD + frames :, :] = edge[0]
        stage(x_ref, 0)
        begin(dy_ref, 0, 0, frames)
        turn(0)

    @pl.when(jnp.logical_not(live))
    def _():
        out_ref[...] = x_ref[...]
        gx_ref[...] = dy_ref[...]

    @pl.when(live)
    def _():
        stage(xn_ref, then)
        for j in range(0, hid, hid_chunk):
            cols = slice(j, j + hid_chunk)
            h = dot_nn(nb[now], w_in_ref[:, cols]) + ib_ref[0:1, cols]
            u = h * ROOT_HALF
            cdf = 0.5 * lax.erf(u) + 0.5
            slope = cdf + h * (jnp.exp2(u * u * (-LOG2E)) * INV_ROOT_2PI)
            acts[0, :, cols] = (h * cdf).astype(BF16)
            ga = dot_nt(gob[now], w_out_ref[cols, :])
            gh = (ga * slope).astype(BF16)
            acts[1, :, cols] = gh
            acc_ib[:, cols] += fold8(gh.astype(F32))

        wide = 256
        tall = frames // (2 * (chans // wide))
        for c in range(0, chans, wide):
            spot = 2 * (c // wide) * tall
            gn[:, c : c + wide] = dot_nt(acts[1], w_in_ref[c : c + wide, :])
            begin(dyn_ref, then, spot, tall)
            raw[:, c : c + wide] = dot_nn(acts[0], w_out_ref[:, c : c + wide])
            begin(dyn_ref, then, spot + tall, tall)
        turn(then)

        rows_each = frames // parts
        units = 2 * (hid // hid_chunk)

        def norm_back(base):
            at_rows = pl.ds(base, rows_each)
            hats = [xh[now, g, at_rows, :] for g in range(groups)]
            grads = [gn[at_rows, span[g]] for g in range(groups)]
            gained = []
            for g in range(groups):
                acc_small[shift, :, span[g]] += fold8(grads[g])
                acc_small[gain, :, span[g]] += fold8(grads[g] * hats[g])
                gained.append(grads[g] * row(gain, g))
            mean = total(gained)
            slant = total([v * h for v, h in zip(gained, hats)])
            inv = rs[now, at_rows, :]
            for g in range(groups):
                gmix = inv * (gained[g] - mean - hats[g] * slant)
                acc_small[taps, :, span[g]] += fold8(gmix)
                gm[g, pl.ds(base + PAD, rows_each), :] = gmix

        def finish(base):
            at_rows = pl.ds(base, rows_each)
            for g in range(groups):
                o = raw[at_rows, span[g]] + row(obias, g)
                dy = dy_ref[0, at_rows, span[g]].astype(F32)
                acc_small[scale, :, span[g]] += fold8(dy * o)
                acc_small[obias, :, span[g]] += fold8(gob[now, at_rows, span[g]].astype(F32))
                x = xp[now, g, pl.ds(base + PAD, rows_each), :]
                out_ref[0, at_rows, span[g]] = (x + o * row(scale, g)).astype(BF16)

        def conv_back(base):
            at_rows = pl.ds(base, rows_each)
            for g in range(groups):
                x = xp[now, g, pl.ds(base + PAD, rows_each), :]
                grad = dy_ref[0, at_rows, span[g]].astype(F32)
                for k in range(taps):
                    moved = gm[g, pl.ds(base + (PAD + margin - k), rows_each), :]
                    grad = grad + moved * row(k, g)
                    acc_small[k, :, span[g]] += fold8(moved * x)
                gx_ref[0, at_rows, span[g]] = grad.astype(BF16)

        def weights(unit):
            side, place = unit % 2, unit // 2
            cols = slice(place * hid_chunk, (place + 1) * hid_chunk)
            acc[side, :, cols] += dot_nn(left[now, side], acts[side, :, cols])

        done = 0
        for i in range(parts):
            upto = units * (i + 1) // parts
            norm_back(i * rows_each)
            for unit in range(done, upto):
                weights(unit)
            done = upto
            finish(i * rows_each)
            if i > 0:
                conv_back((i - 1) * rows_each)
        conv_back(frames - rows_each)

    @pl.when(step == pl.num_programs(0) - 1)
    def _():
        gin_ref[...] = acc[1].astype(gin_ref.dtype)
        for j in range(0, hid, 128):
            gout_ref[j : j + 128, :] = acc[0, :, j : j + 128].T.astype(gout_ref.dtype)
        pack_small(acc_small, acc_ib, rows_ref, small_ref)


def clip_call(counts, x, dy, w_in, w_out, pieces, taps, grad_dtype=BF16):
    clips, frames, chans = x.shape
    hid = w_in.shape[1]
    slots = clips // counts.shape[0]
    kinds = taps + 5

    def clip_spec(ahead):
        def index(i, counts):
            return clip_of(jnp.minimum(i + ahead, clips - 1), counts, slots), 0, 0

        return pl.BlockSpec((1, frames, chans), index)

    def whole(shape):
        return pl.BlockSpec(shape, lambda i, counts: (0,) * len(shape), pipeline_mode=pl.Buffered(1))

    groups = chans // 128
    return pl.pallas_call(
        partial(clip_kernel, taps=taps, hid_chunk=256, row_chunk=32, parts=8),
        out_shape=(
            jax.ShapeDtypeStruct(x.shape, BF16),
            jax.ShapeDtypeStruct(x.shape, BF16),
            jax.ShapeDtypeStruct((chans, hid), grad_dtype),
            jax.ShapeDtypeStruct((hid, chans), grad_dtype),
            jax.ShapeDtypeStruct(pieces.shape, F32),
        ),
        grid_spec=pltpu.PrefetchScalarGridSpec(
            num_scalar_prefetch=1,
            grid=(clips,),
            in_specs=[
                clip_spec(0),
                clip_spec(0),
                clip_spec(1),
                clip_spec(1),
                whole((chans, hid)),
                whole((hid, chans)),
                whole(pieces.shape),
            ],
            out_specs=(
                clip_spec(0),
                clip_spec(0),
                whole((chans, hid)),
                whole((hid, chans)),
                whole(pieces.shape),
            ),
            scratch_shapes=[
                pltpu.VMEM((16, chans), F32),
                pltpu.VMEM((8, hid), F32),
                pltpu.VMEM((2, groups, frames + 2 * PAD, 128), F32),
                pltpu.VMEM((groups, frames + 2 * PAD, 128), F32),
                pltpu.VMEM((2, groups, frames, 128), F32),
                pltpu.VMEM((2, frames, 128), F32),
                pltpu.VMEM((2, 2, chans, frames), BF16),
                pltpu.VMEM((2, frames, hid), BF16),
                pltpu.VMEM((2, frames, chans), BF16),
                pltpu.VMEM((2, frames, chans), BF16),
                pltpu.VMEM((frames, chans), F32),
                pltpu.VMEM((frames, chans), F32),
                pltpu.VMEM((2, chans, hid), F32),
                pltpu.VMEM((kinds, 8, chans), F32),
                pltpu.VMEM((8, hid), F32),
            ],
        ),
        compiler_params=pltpu.CompilerParams(vmem_limit_bytes=60 << 20),
        name="clips",
    )(counts, x, dy, x, dy, w_in, w_out, pieces)


MESH = pl.DeviceIdType.MESH


def grid_of(mesh_shape):
    across = mesh_shape["dp"] // 2
    deep = mesh_shape["fsdp"]
    tall = across if deep % across == 0 else 1
    return across, tall, deep // tall


def place(sizes):
    dp = lax.axis_index("dp")
    fsdp = lax.axis_index("fsdp")
    return dp // 2, dp % 2, fsdp // sizes[1], fsdp % sizes[1]


def at(sizes, x, core, z, y):
    return {"dp": x * 2 + core, "fsdp": z * sizes[1] + y}


def partners(sizes):
    x, core, z, y = place(sizes)
    across, tall, deep = sizes
    found = [at(sizes, x, 1 - core, z, y)]
    found += [at(sizes, (x + o) % across, core, z, y) for o in range(1, across)]
    found += [at(sizes, x, core, z, (y + o) % tall) for o in range(1, tall)]
    found += [at(sizes, x, core, (z + o) % deep, y) for o in range(1, deep)]
    return found


def greet(sizes):
    barrier = pltpu.get_barrier_semaphore()
    others = partners(sizes)
    for other in others:
        pl.semaphore_signal(barrier, inc=1, device_id=other, device_id_type=MESH)
    pl.semaphore_wait(barrier, len(others))


def send(src, dst, send_sems, recv_sems, slot, device):
    copy = pltpu.make_async_remote_copy(
        src_ref=src,
        dst_ref=dst,
        send_sem=send_sems.at[slot],
        recv_sem=recv_sems.at[slot],
        device_id=device,
        device_id_type=MESH,
    )
    copy.start()
    return copy


class Slots:
    def __init__(self):
        self.used = 0

    def take(self):
        self.used += 1
        return self.used - 1


def gather_copies(sizes):
    across, tall, deep = sizes
    columns = across * tall
    return 3 * ((deep - 1) + (columns - 1) + columns)


def gather_kernel(small_ref, in_ref, out_ref, full_small, full_in, full_out, send_sems, recv_sems, local_sems, *, sizes):
    across, tall, deep = sizes
    x, core, z, y = place(sizes)
    slots = Slots()
    greet(sizes)
    own = (small_ref, in_ref, out_ref)
    full = (full_small, full_in, full_out)
    x_first = (True, True, False)

    lines = []
    keeps = []
    for i in range(3):
        keep = pltpu.make_async_copy(own[i], full[i].at[x, core, z, y], local_sems.at[i])
        keep.start()
        keeps.append(keep)
        line = []
        for o in range(1, deep):
            line.append(
                send(own[i], full[i].at[x, core, z, y], send_sems, recv_sems, slots.take(), at(sizes, x, core, (z + o) % deep, y))
            )
        lines.append(line)
    started = [c for line in lines for c in line]

    def column(i, cx, cy):
        return full[i].at[cx, core, :, cy]

    def move(i, cx, cy, device):
        copy = send(column(i, cx, cy), column(i, cx, cy), send_sems, recv_sems, slots.take(), device)
        started.append(copy)
        return copy

    firsts, seconds, sides = [], [], []
    for i in range(3):
        keeps[i].wait()
        for copy in lines[i]:
            copy.wait_recv()
        along_x = [move(i, x, y, at(sizes, (x + o) % across, core, z, y)) for o in range(1, across)]
        along_y = [move(i, x, y, at(sizes, x, core, z, (y + o) % tall)) for o in range(1, tall)]
        firsts.append((along_x, along_y))
        sides.append(move(i, x, y, at(sizes, x, 1 - core, z, y)))
    for i in range(3):
        along_x, along_y = firsts[i]
        passed = []
        if x_first[i]:
            for o, copy in zip(range(1, across), along_x):
                copy.wait_recv()
                cx = (x - o + across) % across
                passed.append([move(i, cx, y, at(sizes, x, core, z, (y + p) % tall)) for p in range(1, tall)])
                sides.append(move(i, cx, y, at(sizes, x, 1 - core, z, y)))
            for o, copy in zip(range(1, tall), along_y):
                copy.wait_recv()
                sides.append(move(i, x, (y - o + tall) % tall, at(sizes, x, 1 - core, z, y)))
        else:
            for o, copy in zip(range(1, tall), along_y):
                copy.wait_recv()
                cy = (y - o + tall) % tall
                passed.append([move(i, x, cy, at(sizes, (x + p) % across, core, z, y)) for p in range(1, across)])
                sides.append(move(i, x, cy, at(sizes, x, 1 - core, z, y)))
            for o, copy in zip(range(1, across), along_x):
                copy.wait_recv()
                sides.append(move(i, (x - o + across) % across, y, at(sizes, x, 1 - core, z, y)))
        seconds.append(passed)
    for i in range(3):
        for o, row in enumerate(seconds[i], 1):
            for p, copy in enumerate(row, 1):
                copy.wait_recv()
                if x_first[i]:
                    cx, cy = (x - o + across) % across, (y - p + tall) % tall
                else:
                    cx, cy = (x - p + across) % across, (y - o + tall) % tall
                sides.append(move(i, cx, cy, at(sizes, x, 1 - core, z, y)))
    for copy in sides:
        copy.wait_recv()
    for copy in started:
        copy.wait_send()


def gather_call(sizes, small, w_in, w_out):
    across, tall, deep = sizes
    copies = gather_copies(sizes)
    shards = (small, w_in, w_out)
    vmem = pl.BlockSpec(memory_space=pltpu.VMEM)
    return pl.pallas_call(
        partial(gather_kernel, sizes=sizes),
        out_shape=tuple(jax.ShapeDtypeStruct((across, 2, deep, tall) + s.shape, s.dtype) for s in shards),
        in_specs=[vmem] * 3,
        out_specs=(pl.BlockSpec(memory_space=pl.ANY),) * 3,
        scratch_shapes=[
            pltpu.SemaphoreType.DMA((copies,)),
            pltpu.SemaphoreType.DMA((copies,)),
            pltpu.SemaphoreType.DMA((3,)),
        ],
        compiler_params=pltpu.CompilerParams(collective_id=0, has_side_effects=True),
        name="gather",
    )(*shards)


def scatter_copies(sizes):
    across, tall, deep = sizes
    columns = across * tall
    return 3 * (columns + (columns - 1) + (deep - 1))


def add_into(dst, terms):
    def block(k, carry):
        total = terms[0][k].astype(F32)
        for term in terms[1:]:
            total = total + term[k].astype(F32)
        dst[k] = total.astype(dst.dtype)
        return carry

    lax.fori_loop(0, dst.shape[0], block, 0)


def scatter_kernel(*refs, sizes):
    across, tall, deep = sizes
    parts = refs[0:3]
    outs = refs[3:6]
    side = refs[6:9]
    held = refs[9:12]
    corner = refs[12:15]
    mixed = refs[15:18]
    direct = refs[18:21]
    routed = refs[21:24]
    total = refs[24:27]
    lines = refs[27:30]
    send_sems, recv_sems = refs[30:32]
    x, core, z, y = place(sizes)
    slots = Slots()
    greet(sizes)
    x_first = (True, True, False)
    started = []

    def move(src, dst, device):
        copy = send(src, dst, send_sems, recv_sems, slots.take(), device)
        started.append(copy)
        return copy

    def far(i, a, b):
        if x_first[i]:
            return (x + a) % across, (y + b) % tall
        return (x + b) % across, (y + a) % tall

    def lengths(i):
        return (across, tall) if x_first[i] else (tall, across)

    def peer(i, a, b):
        cx, cy = far(i, a, b)
        return at(sizes, cx, core, z, cy)

    order = {}
    for i in range(3):
        last, first = lengths(i)
        order[i] = [(a, b) for a in range(1, last) for b in range(1, first)]
        order[i] += [(0, b) for b in range(1, first)]
        order[i] += [(a, 0) for a in range(1, last)] + [(0, 0)]
    crossings = {}
    for k in range(across * tall):
        for i in range(3):
            cx, cy = far(i, *order[i][k])
            crossings[i, order[i][k]] = move(
                parts[i].at[cx, 1 - core, :, cy], side[i].at[cx, cy], at(sizes, x, 1 - core, z, y)
            )

    def own(i, a, b):
        cx, cy = far(i, a, b)
        crossings[i, (a, b)].wait_recv()
        add_into(held[i].at[cx, cy], [parts[i].at[cx, core, :, cy], side[i].at[cx, cy]])
        return held[i].at[cx, cy]

    corners, directs, routeds = {}, {}, {}
    for i in range(3):
        last, first = lengths(i)
        for a in range(1, last):
            for b in range(1, first):
                src = own(i, a, b)
                corners[i, a, b] = move(src, corner[i].at[a - 1, b - 1], peer(i, 0, b))
    for i in range(3):
        last, first = lengths(i)
        for b in range(1, first):
            src = own(i, 0, b)
            directs[i, b] = move(src, direct[i].at[b - 1], peer(i, 0, b))
    for i in range(3):
        last, first = lengths(i)
        for a in range(1, last):
            src = own(i, a, 0)
            terms = [src]
            for b in range(1, first):
                corners[i, a, b].wait_recv()
                terms.append(corner[i].at[a - 1, b - 1])
            add_into(mixed[i].at[a - 1], terms)
            routeds[i, a] = move(mixed[i].at[a - 1], routed[i].at[a - 1], peer(i, a, 0))
    ends = {}
    for i in range(3):
        last, first = lengths(i)
        terms = [own(i, 0, 0)]
        for b in range(1, first):
            directs[i, b].wait_recv()
            terms.append(direct[i].at[b - 1])
        for a in range(1, last):
            routeds[i, a].wait_recv()
            terms.append(routed[i].at[a - 1])
        add_into(total[i], terms)
        for o in range(1, deep):
            ends[i, o] = move(
                total[i].at[(z + o) % deep], lines[i].at[o - 1], at(sizes, x, core, (z + o) % deep, y)
            )
    for i in range(3):
        value = total[i][z].astype(F32)
        for o in range(1, deep):
            ends[i, o].wait_recv()
            value = value + lines[i][o - 1].astype(F32)
        outs[i][...] = value
    for copy in started:
        copy.wait_send()


def scatter_call(sizes, small, g_in, g_out):
    across, tall, deep = sizes
    copies = scatter_copies(sizes)
    parts = (small, g_in, g_out)
    vmem = pl.BlockSpec(memory_space=pltpu.VMEM)
    pieces = [p.shape[4:] for p in parts]
    kinds = [p.dtype for p in parts]

    def scratch(lead):
        return [pltpu.VMEM(lead(i) + pieces[i], kinds[i]) for i in range(3)]

    last = (across, across, tall)
    first = (tall, tall, across)
    grid = lambda i: (across, tall, deep)
    return pl.pallas_call(
        partial(scatter_kernel, sizes=sizes),
        out_shape=tuple(jax.ShapeDtypeStruct(p, F32) for p in pieces),
        in_specs=[vmem] * 3,
        out_specs=(vmem,) * 3,
        scratch_shapes=[
            *scratch(grid),
            *scratch(grid),
            *scratch(lambda i: (max(last[i] - 1, 1), max(first[i] - 1, 1), deep)),
            *scratch(lambda i: (max(last[i] - 1, 1), deep)),
            *scratch(lambda i: (max(first[i] - 1, 1), deep)),
            *scratch(lambda i: (max(last[i] - 1, 1), deep)),
            *scratch(lambda i: (deep,)),
            *scratch(lambda i: (max(deep - 1, 1),)),
            pltpu.SemaphoreType.DMA((copies,)),
            pltpu.SemaphoreType.DMA((copies,)),
        ],
        compiler_params=pltpu.CompilerParams(collective_id=1, has_side_effects=True, vmem_limit_bytes=60 << 20),
        name="scatter",
    )(*parts)


def on_device(
    mel_clips,
    live_counts,
    conv_weight,
    conv_bias,
    norm_gain,
    norm_shift,
    in_weight,
    in_bias,
    out_weight,
    out_bias,
    layer_scale,
    cotangent,
    *,
    sizes,
):
    shard, taps = conv_weight.shape
    kinds = taps + 5
    hid = in_weight.shape[1]
    devices = lax.axis_size(("dp", "fsdp"))
    chans = shard * devices
    wide = in_bias.shape[0]
    lead = (sizes[0], 2, sizes[2], sizes[1])

    lines = jnp.stack([conv_bias, norm_gain, norm_shift, out_bias, layer_scale])
    lines = jnp.pad(jnp.concatenate([conv_weight.T, lines]), ((0, 0), (0, 128 - shard)))
    last = jnp.pad(in_bias[None, :], ((0, 15 - kinds), (0, 128 - wide)))
    small, full_in, full_out = gather_call(sizes, jnp.concatenate([lines, last]), in_weight, out_weight)
    block_out, grad_clips, grad_in, grad_out, small = clip_call(
        live_counts.reshape(-1),
        mel_clips,
        cotangent,
        full_in.reshape(chans, hid),
        full_out.reshape(hid, chans),
        small.reshape(devices, 16, 128),
        taps,
    )
    small, grad_in, grad_out = scatter_call(
        sizes,
        small.reshape(lead + (16, 128)),
        grad_in.reshape(lead + in_weight.shape),
        grad_out.reshape(lead + out_weight.shape),
    )
    return (
        block_out,
        grad_clips,
        small[:taps, :shard].T,
        small[taps, :shard],
        small[taps + 1, :shard],
        small[taps + 2, :shard],
        grad_in,
        small[kinds, :wide],
        grad_out,
        small[taps + 3, :shard],
        small[taps + 4, :shard],
    )


def solution(mesh):
    both = ("dp", "fsdp")
    row, mat, cube = P(both), P(both, None), P(both, None, None)
    in_specs = (cube, mat, mat, row, row, row, mat, row, mat, row, row, cube)
    out_specs = (cube, cube, mat, row, row, row, mat, row, mat, row, row)
    body = partial(on_device, sizes=grid_of(mesh.shape))
    return jax.shard_map(body, mesh=mesh, in_specs=in_specs, out_specs=out_specs, check_vma=False)
```

profile of v0, /device:TPU:0, one launch (start us, length us, event | category | flops | bytes accessed | tf_op | source)
XLA Modules:
  0.0 157.3 jit_solution(15243843612597672377)
XLA Ops:
  0.6 1.4 concatenate.6
  2.1 1.3 fusion.2.small_ref
  3.3 30.7 %gather.1 = (bf16[2,2,4,2,16,128]{5,4,3,2,1,0:T(8,128)(2,1)}, bf16[2,2,4,2,16,1536]{5,4,3,2,1,0:T(8,128)(2,1)}, bf16[2,2,4,2,48,512]{5,4,3,2,1,0:T(8,128)(2,1)}) custom-call(bf16[16,128]{1,0:T(8,128)(2,1)} %fusion.2.small_ref, bf16[16,1536]{1,0:T(8,128)(2,1)} %in_ref.1, bf16[48,512]{1,0:T(8,128)(2,1)} %out_ref.1), custom_call_target="tpu_custom_call" | custom-call | tf_op jit(solution)/shard_map/gather/pallas_call | solution.py:508
  34.1 83.7 %clips.1 = (bf16[20,256,512]{2,1,0:T(8,128)(2,1)}, bf16[20,256,512]{2,1,0:T(8,128)(2,1)}, bf16[512,1536]{1,0:T(8,128)(2,1)}, bf16[1536,512]{1,0:T(8,128)(2,1)}, f32[32,16,128]{2,1,0:T(8,128)}) custom-call(s32[4]{0:T(128)} %bitcast.35, bf16[20,256,512]{2,1,0:T(8,128)(2,1)} %xn_ref.1, bf16[20,256,512]{2,1,0:T(8,128)(2,1)} %dyn_ref.1, ...), custom_call_target="tpu_custom_call" | custom-call | tf_op jit(solution)/shard_map/clips/pallas_call | solution.py:309
  117.7 32.6 %scatter.1 = (f32[16,128]{1,0:T(8,128)}, f32[16,1536]{1,0:T(8,128)}, f32[48,512]{1,0:T(8,128)}) custom-call(f32[2,2,4,2,16,128]{5,4,3,2,1,0:T(8,128)} %bitcast.32, bf16[2,2,4,2,16,1536]{5,4,3,2,1,0:T(8,128)(2,1)} %bitcast.28, bf16[2,2,4,2,48,512]{5,4,3,2,1,0:T(8,128)(2,1)} %bitcast.29), custom_call_target="tpu_custom_call" | custom-call | tf_op jit(solution)/shard_map/scatter/pallas_call | solution.py:657
  150.4 1.2 slice_bitcast_fusion.3
  151.6 1.4 slice_bitcast_fusion.1
  152.9 1.3 slice_bitcast_fusion
  154.2 1.5 copy.25
  155.8 1.5 copy.26
where the time goes:
time: 160 us; the launch traced here: 157 us
  Pallas kernels  147 us (92%)
  local copies, waits for them, and re-layouts  8.34 us (5%)
    pallas_call x1, Pallas kernels, clip_call(): pl.pallas_call(partial(clip_kernel, taps=taps, hid_chunk=256, row_chunk=3...  83.7 us
    pallas_call x1, Pallas kernels, scatter_call(): pl.pallas_call(partial(scatter_kernel, sizes=sizes), out_shape=tuple((jax...  32.6 us
    pallas_call x1, Pallas kernels, gather_call(): pl.pallas_call(partial(gather_kernel, sizes=sizes), out_shape=tuple((jax....  30.7 us

commit v1 on v0

--- a/solution.py
+++ b/solution.py
@@ -95,6 +95,7 @@
 
 def clip_kernel(
     counts_ref,
+    order_ref,
     x_ref,
     dy_ref,
     xn_ref,
@@ -290,20 +291,19 @@
         pack_small(acc_small, acc_ib, rows_ref, small_ref)
 
 
-def clip_call(counts, x, dy, w_in, w_out, pieces, taps, grad_dtype=BF16):
+def clip_call(counts, order, x, dy, w_in, w_out, pieces, taps, grad_dtype=BF16):
     clips, frames, chans = x.shape
     hid = w_in.shape[1]
-    slots = clips // counts.shape[0]
     kinds = taps + 5
 
     def clip_spec(ahead):
-        def index(i, counts):
-            return clip_of(jnp.minimum(i + ahead, clips - 1), counts, slots), 0, 0
+        def index(i, counts, order):
+            return order[jnp.minimum(i + ahead, clips - 1)], 0, 0
 
         return pl.BlockSpec((1, frames, chans), index)
 
     def whole(shape):
-        return pl.BlockSpec(shape, lambda i, counts: (0,) * len(shape), pipeline_mode=pl.Buffered(1))
+        return pl.BlockSpec(shape, lambda i, counts, order: (0,) * len(shape), pipeline_mode=pl.Buffered(1))
 
     groups = chans // 128
     return pl.pallas_call(
@@ -316,7 +316,7 @@
             jax.ShapeDtypeStruct(pieces.shape, F32),
         ),
         grid_spec=pltpu.PrefetchScalarGridSpec(
-            num_scalar_prefetch=1,
+            num_scalar_prefetch=2,
             grid=(clips,),
             in_specs=[
                 clip_spec(0),
@@ -354,7 +354,7 @@
         ),
         compiler_params=pltpu.CompilerParams(vmem_limit_bytes=60 << 20),
         name="clips",
-    )(counts, x, dy, x, dy, w_in, w_out, pieces)
+    )(counts, order, x, dy, x, dy, w_in, w_out, pieces)
 
 
 MESH = pl.DeviceIdType.MESH
@@ -417,113 +417,150 @@
         return self.used - 1
 
 
-def gather_copies(sizes):
+def streams_of(refs_in, refs_full, cuts):
+    widths = [r.shape[-1] for r in refs_in]
+    found = [[(0, slice(0, widths[0]), True)]] + [[] for _ in range(cuts - 1)]
+    for c in range(cuts):
+        for i, x_first in ((1, True), (2, False)):
+            each = widths[i] // cuts
+            found[c].append((i, slice(c * each, (c + 1) * each), x_first))
+    return found
+
+
+def copies_of(sizes, streams):
     across, tall, deep = sizes
     columns = across * tall
-    return 3 * ((deep - 1) + (columns - 1) + columns)
-
-
-def gather_kernel(small_ref, in_ref, out_ref, full_small, full_in, full_out, send_sems, recv_sems, local_sems, *, sizes):
+    return streams * ((deep - 1) + (columns - 1) + columns)
+
+
+def gather_kernel(*refs, sizes, cuts, slots, kinds):
     across, tall, deep = sizes
+    counts_ref, conv_ref = refs[0:2]
+    vectors = refs[2:7]
+    bias_ref, in_ref, out_ref, full_small, full_in, full_out, order_ref = refs[7:14]
+    tile, small_ref, send_sems, recv_sems, local_sems = refs[14:]
     x, core, z, y = place(sizes)
-    slots = Slots()
+    slots_used = Slots()
+    started = []
     greet(sizes)
+    tile[...] = jnp.zeros_like(tile)
+    taps, shard = conv_ref.shape
+    tile[0:taps, 0:shard] = conv_ref[...].astype(F32)
+    for k, vector in enumerate(vectors):
+        tile[taps + k : taps + k + 1, 0:shard] = vector[...].astype(F32)
+    tile[kinds : kinds + 1, 0 : bias_ref.shape[1]] = bias_ref[...].astype(F32)
+    small_ref[...] = tile[...].astype(BF16)
+
     own = (small_ref, in_ref, out_ref)
     full = (full_small, full_in, full_out)
-    x_first = (True, True, False)
-
-    lines = []
+    groups = streams_of(own, full, cuts)
+
+    def move(src, dst, device):
+        copy = send(src, dst, send_sems, recv_sems, slots_used.take(), device)
+        started.append(copy)
+        return copy
+
+    def column(stream, cx, cy):
+        i, cols, _ = stream
+        return full[i].at[cx, core, :, cy, :, cols]
+
+    def along(stream, cx, cy, device):
+        ref = column(stream, cx, cy)
+        return move(ref, ref, device)
+
+    def beside(stream, cx, cy):
+        sides.append(along(stream, cx, cy, at(sizes, x, 1 - core, z, y)))
+
     keeps = []
-    for i in range(3):
+    lines = {}
+    sides = []
+    for i in (1, 2, 0):
         keep = pltpu.make_async_copy(own[i], full[i].at[x, core, z, y], local_sems.at[i])
         keep.start()
         keeps.append(keep)
-        line = []
-        for o in range(1, deep):
-            line.append(
-                send(own[i], full[i].at[x, core, z, y], send_sems, recv_sems, slots.take(), at(sizes, x, core, (z + o) % deep, y))
+    for c in range(cuts):
+        for s, (i, cols, _) in enumerate(groups[c]):
+            lines[c, s] = [
+                move(
+                    own[i].at[:, cols],
+                    full[i].at[x, core, z, y, :, cols],
+                    at(sizes, x, core, (z + o) % deep, y),
+                )
+                for o in range(1, deep)
+            ]
+    for k in range(order_ref.shape[0]):
+        order_ref[k] = clip_of(jnp.int32(k), counts_ref, slots)
+    for keep in keeps:
+        keep.wait()
+    firsts = {}
+    for c in range(cuts):
+        for s, stream in enumerate(groups[c]):
+            for copy in lines[c, s]:
+                copy.wait_recv()
+            firsts[c, s] = (
+                [along(stream, x, y, at(sizes, (x + o) % across, core, z, y)) for o in range(1, across)],
+                [along(stream, x, y, at(sizes, x, core, z, (y + o) % tall)) for o in range(1, tall)],
             )
-        lines.append(line)
-    started = [c for line in lines for c in line]
-
-    def column(i, cx, cy):
-        return full[i].at[cx, core, :, cy]
-
-    def move(i, cx, cy, device):
-        copy = send(column(i, cx, cy), column(i, cx, cy), send_sems, recv_sems, slots.take(), device)
-        started.append(copy)
-        return copy
-
-    firsts, seconds, sides = [], [], []
-    for i in range(3):
-        keeps[i].wait()
-        for copy in lines[i]:
-            copy.wait_recv()
-        along_x = [move(i, x, y, at(sizes, (x + o) % across, core, z, y)) for o in range(1, across)]
-        along_y = [move(i, x, y, at(sizes, x, core, z, (y + o) % tall)) for o in range(1, tall)]
-        firsts.append((along_x, along_y))
-        sides.append(move(i, x, y, at(sizes, x, 1 - core, z, y)))
-    for i in range(3):
-        along_x, along_y = firsts[i]
-        passed = []
-        if x_first[i]:
-            for o, copy in zip(range(1, across), along_x):
+            beside(stream, x, y)
+    passed = {}
+    for c in range(cuts):
+        for s, stream in enumerate(groups[c]):
+            along_x, along_y = firsts[c, s]
+            lead, other = (along_x, along_y) if stream[2] else (along_y, along_x)
+            passed[c, s] = []
+            for o, copy in enumerate(lead, 1):
                 copy.wait_recv()
-                cx = (x - o + across) % across
-                passed.append([move(i, cx, y, at(sizes, x, core, z, (y + p) % tall)) for p in range(1, tall)])
-                sides.append(move(i, cx, y, at(sizes, x, 1 - core, z, y)))
-            for o, copy in zip(range(1, tall), along_y):
+                if stream[2]:
+                    cx, cy = (x - o + across) % across, y
+                    goals = [at(sizes, x, core, z, (y + p) % tall) for p in range(1, tall)]
+                else:
+                    cx, cy = x, (y - o + tall) % tall
+                    goals = [at(sizes, (x + p) % across, core, z, y) for p in range(1, across)]
+                passed[c, s].append([along(stream, cx, cy, goal) for goal in goals])
+                beside(stream, cx, cy)
+            for o, copy in enumerate(other, 1):
                 copy.wait_recv()
-                sides.append(move(i, x, (y - o + tall) % tall, at(sizes, x, 1 - core, z, y)))
-        else:
-            for o, copy in zip(range(1, tall), along_y):
-                copy.wait_recv()
-                cy = (y - o + tall) % tall
-                passed.append([move(i, x, cy, at(sizes, (x + p) % across, core, z, y)) for p in range(1, across)])
-                sides.append(move(i, x, cy, at(sizes, x, 1 - core, z, y)))
-            for o, copy in zip(range(1, across), along_x):
-                copy.wait_recv()
-                sides.append(move(i, (x - o + across) % across, y, at(sizes, x, 1 - core, z, y)))
-        seconds.append(passed)
-    for i in range(3):
-        for o, row in enumerate(seconds[i], 1):
-            for p, copy in enumerate(row, 1):
-                copy.wait_recv()
-                if x_first[i]:
-                    cx, cy = (x - o + across) % across, (y - p + tall) % tall
+                if stream[2]:
+                    beside(stream, x, (y - o + tall) % tall)
                 else:
-                    cx, cy = (x - p + across) % across, (y - o + tall) % tall
-                sides.append(move(i, cx, cy, at(sizes, x, 1 - core, z, y)))
+                    beside(stream, (x - o + across) % across, y)
+    for c in range(cuts):
+        for s, stream in enumerate(groups[c]):
+            for o, goals in enumerate(passed[c, s], 1):
+                for p, copy in enumerate(goals, 1):
+                    copy.wait_recv()
+                    dx, dy = (o, p) if stream[2] else (p, o)
+                    beside(stream, (x - dx + across) % across, (y - dy + tall) % tall)
     for copy in sides:
         copy.wait_recv()
     for copy in started:
         copy.wait_send()
 
 
-def gather_call(sizes, small, w_in, w_out):
+def gather_call(sizes, counts, clips, conv, vectors, bias, w_in, w_out):
     across, tall, deep = sizes
-    copies = gather_copies(sizes)
-    shards = (small, w_in, w_out)
+    cuts = 2
+    copies = copies_of(sizes, 2 * cuts + 1)
     vmem = pl.BlockSpec(memory_space=pltpu.VMEM)
+    smem = pl.BlockSpec(memory_space=pltpu.SMEM)
+    shapes = ((16, 128), w_in.shape, w_out.shape)
+    kinds = conv.shape[0] + len(vectors)
     return pl.pallas_call(
-        partial(gather_kernel, sizes=sizes),
-        out_shape=tuple(jax.ShapeDtypeStruct((across, 2, deep, tall) + s.shape, s.dtype) for s in shards),
-        in_specs=[vmem] * 3,
-        out_specs=(pl.BlockSpec(memory_space=pl.ANY),) * 3,
+        partial(gather_kernel, sizes=sizes, cuts=cuts, slots=clips // counts.shape[0], kinds=kinds),
+        out_shape=tuple(jax.ShapeDtypeStruct((across, 2, deep, tall) + s, BF16) for s in shapes)
+        + (jax.ShapeDtypeStruct((clips,), jnp.int32),),
+        in_specs=[smem] + [vmem] * (len(vectors) + 4),
+        out_specs=(pl.BlockSpec(memory_space=pl.ANY),) * 3 + (smem,),
         scratch_shapes=[
+            pltpu.VMEM((16, 128), F32),
+            pltpu.VMEM((16, 128), BF16),
             pltpu.SemaphoreType.DMA((copies,)),
             pltpu.SemaphoreType.DMA((copies,)),
             pltpu.SemaphoreType.DMA((3,)),
         ],
         compiler_params=pltpu.CompilerParams(collective_id=0, has_side_effects=True),
         name="gather",
-    )(*shards)
-
-
-def scatter_copies(sizes):
-    across, tall, deep = sizes
-    columns = across * tall
-    return 3 * (columns + (columns - 1) + (deep - 1))
+    )(counts, conv, *vectors, bias, w_in, w_out)
 
 
 def add_into(dst, terms):
@@ -537,7 +574,7 @@
     lax.fori_loop(0, dst.shape[0], block, 0)
 
 
-def scatter_kernel(*refs, sizes):
+def scatter_kernel(*refs, sizes, cuts):
     across, tall, deep = sizes
     parts = refs[0:3]
     outs = refs[3:6]
@@ -551,98 +588,138 @@
     lines = refs[27:30]
     send_sems, recv_sems = refs[30:32]
     x, core, z, y = place(sizes)
-    slots = Slots()
+    slots_used = Slots()
     greet(sizes)
-    x_first = (True, True, False)
     started = []
+    groups = streams_of(parts, outs, cuts)
 
     def move(src, dst, device):
-        copy = send(src, dst, send_sems, recv_sems, slots.take(), device)
+        copy = send(src, dst, send_sems, recv_sems, slots_used.take(), device)
         started.append(copy)
         return copy
 
-    def far(i, a, b):
-        if x_first[i]:
+    def far(stream, a, b):
+        if stream[2]:
             return (x + a) % across, (y + b) % tall
         return (x + b) % across, (y + a) % tall
 
-    def lengths(i):
-        return (across, tall) if x_first[i] else (tall, across)
-
-    def peer(i, a, b):
-        cx, cy = far(i, a, b)
+    def lengths(stream):
+        return (across, tall) if stream[2] else (tall, across)
+
+    def peer(stream, a, b):
+        cx, cy = far(stream, a, b)
         return at(sizes, cx, core, z, cy)
 
-    order = {}
-    for i in range(3):
-        last, first = lengths(i)
-        order[i] = [(a, b) for a in range(1, last) for b in range(1, first)]
-        order[i] += [(0, b) for b in range(1, first)]
-        order[i] += [(a, 0) for a in range(1, last)] + [(0, 0)]
+    def of(group, stream, *index):
+        i, cols, _ = stream
+        return group[i].at[index + (slice(None), slice(None), cols)]
+
     crossings = {}
-    for k in range(across * tall):
-        for i in range(3):
-            cx, cy = far(i, *order[i][k])
-            crossings[i, order[i][k]] = move(
-                parts[i].at[cx, 1 - core, :, cy], side[i].at[cx, cy], at(sizes, x, 1 - core, z, y)
-            )
-
-    def own(i, a, b):
-        cx, cy = far(i, a, b)
-        crossings[i, (a, b)].wait_recv()
-        add_into(held[i].at[cx, cy], [parts[i].at[cx, core, :, cy], side[i].at[cx, cy]])
-        return held[i].at[cx, cy]
-
-    corners, directs, routeds = {}, {}, {}
-    for i in range(3):
-        last, first = lengths(i)
-        for a in range(1, last):
+
+    def cross(c, s, a, b):
+        stream = groups[c][s]
+        cx, cy = far(stream, a, b)
+        i, cols, _ = stream
+        crossings[c, s, a, b] = move(
+            parts[i].at[cx, 1 - core, :, cy, :, cols],
+            of(side, stream, cx, cy),
+            at(sizes, x, 1 - core, z, y),
+        )
+
+    every = [(c, s) for c in range(cuts) for s in range(len(groups[c]))]
+    for c in range(cuts):
+        for kind in range(4):
+            for s, stream in enumerate(groups[c]):
+                last, first = lengths(stream)
+                if kind == 0:
+                    steps = [(a, b) for a in range(1, last) for b in range(1, first)]
+                elif kind == 1:
+                    steps = [(0, b) for b in range(1, first)]
+                elif kind == 2:
+                    steps = [(a, 0) for a in range(1, last)]
+                else:
+                    steps = [(0, 0)]
+                for a, b in steps:
+                    cross(c, s, a, b)
+
+    def own(c, s, a, b):
+        stream = groups[c][s]
+        i, cols, _ = stream
+        cx, cy = far(stream, a, b)
+        crossings[c, s, a, b].wait_recv()
+        add_into(of(held, stream, cx, cy), [parts[i].at[cx, core, :, cy, :, cols], of(side, stream, cx, cy)])
+        return of(held, stream, cx, cy)
+
+    corners, directs, routeds, ends = {}, {}, {}, {}
+
+    def send_corners(c):
+        for s, stream in enumerate(groups[c]):
+            last, first = lengths(stream)
+            for a in range(1, last):
+                for b in range(1, first):
+                    src = own(c, s, a, b)
+                    corners[c, s, a, b] = move(src, of(corner, stream, a - 1, b - 1), peer(stream, 0, b))
+
+    def send_directs(c):
+        for s, stream in enumerate(groups[c]):
+            for b in range(1, lengths(stream)[1]):
+                src = own(c, s, 0, b)
+                directs[c, s, b] = move(src, of(direct, stream, b - 1), peer(stream, 0, b))
+
+    def send_routeds(c):
+        for s, stream in enumerate(groups[c]):
+            last, first = lengths(stream)
+            for a in range(1, last):
+                terms = [own(c, s, a, 0)]
+                for b in range(1, first):
+                    corners[c, s, a, b].wait_recv()
+                    terms.append(of(corner, stream, a - 1, b - 1))
+                add_into(of(mixed, stream, a - 1), terms)
+                routeds[c, s, a] = move(of(mixed, stream, a - 1), of(routed, stream, a - 1), peer(stream, a, 0))
+
+    def send_ends(c):
+        for s, stream in enumerate(groups[c]):
+            i, cols, _ = stream
+            last, first = lengths(stream)
+            terms = [own(c, s, 0, 0)]
             for b in range(1, first):
-                src = own(i, a, b)
-                corners[i, a, b] = move(src, corner[i].at[a - 1, b - 1], peer(i, 0, b))
-    for i in range(3):
-        last, first = lengths(i)
-        for b in range(1, first):
-            src = own(i, 0, b)
-            directs[i, b] = move(src, direct[i].at[b - 1], peer(i, 0, b))
-    for i in range(3):
-        last, first = lengths(i)
-        for a in range(1, last):
-            src = own(i, a, 0)
-            terms = [src]
-            for b in range(1, first):
-                corners[i, a, b].wait_recv()
-                terms.append(corner[i].at[a - 1, b - 1])
-            add_into(mixed[i].at[a - 1], terms)
-            routeds[i, a] = move(mixed[i].at[a - 1], routed[i].at[a - 1], peer(i, a, 0))
-    ends = {}
-    for i in range(3):
-        last, first = lengths(i)
-        terms = [own(i, 0, 0)]
-        for b in range(1, first):
-            directs[i, b].wait_recv()
-            terms.append(direct[i].at[b - 1])
-        for a in range(1, last):
-            routeds[i, a].wait_recv()
-            terms.append(routed[i].at[a - 1])
-        add_into(total[i], terms)
+                directs[c, s, b].wait_recv()
+                terms.append(of(direct, stream, b - 1))
+            for a in range(1, last):
+                routeds[c, s, a].wait_recv()
+                terms.append(of(routed, stream, a - 1))
+            add_into(of(total, stream), terms)
+            for o in range(1, deep):
+                ends[c, s, o] = move(
+                    total[i].at[(z + o) % deep, :, cols],
+                    lines[i].at[o - 1, :, cols],
+                    at(sizes, x, core, (z + o) % deep, y),
+                )
+
+    send_corners(0)
+    send_directs(0)
+    for c in range(1, cuts):
+        send_corners(c)
+        send_routeds(c - 1)
+        send_directs(c)
+    send_routeds(cuts - 1)
+    for c in range(cuts):
+        send_ends(c)
+    for c, s in every:
+        i, cols, _ = groups[c][s]
+        value = total[i][z, :, cols].astype(F32)
         for o in range(1, deep):
-            ends[i, o] = move(
-                total[i].at[(z + o) % deep], lines[i].at[o - 1], at(sizes, x, core, (z + o) % deep, y)
-            )
-    for i in range(3):
-        value = total[i][z].astype(F32)
-        for o in range(1, deep):
-            ends[i, o].wait_recv()
-            value = value + lines[i][o - 1].astype(F32)
-        outs[i][...] = value
+            ends[c, s, o].wait_recv()
+            value = value + lines[i][o - 1, :, cols].astype(F32)
+        outs[i][:, cols] = value
     for copy in started:
         copy.wait_send()
 
 
 def scatter_call(sizes, small, g_in, g_out):
     across, tall, deep = sizes
-    copies = scatter_copies(sizes)
+    cuts = 2
+    copies = copies_of(sizes, 2 * cuts + 1)
     parts = (small, g_in, g_out)
     vmem = pl.BlockSpec(memory_space=pltpu.VMEM)
     pieces = [p.shape[4:] for p in parts]
@@ -655,7 +732,7 @@
     first = (tall, tall, across)
     grid = lambda i: (across, tall, deep)
     return pl.pallas_call(
-        partial(scatter_kernel, sizes=sizes),
+        partial(scatter_kernel, sizes=sizes, cuts=cuts),
         out_shape=tuple(jax.ShapeDtypeStruct(p, F32) for p in pieces),
         in_specs=[vmem] * 3,
         out_specs=(vmem,) * 3,
@@ -676,6 +753,26 @@
     )(*parts)
 
 
+def close_kernel(small_ref, in_ref, out_ref, *results, taps):
+    conv, bias, g_in, g_out = results[0], results[6], results[7], results[8]
+    shard = conv.shape[1]
+    conv[...] = small_ref[0:taps, 0:shard]
+    for k in range(5):
+        results[1 + k][...] = small_ref[taps + k : taps + k + 1, 0:shard]
+    bias[...] = small_ref[taps + 5 : taps + 6, 0 : bias.shape[1]]
+    g_in[...] = in_ref[...]
+    g_out[...] = out_ref[...]
+
+
+def close_call(small, g_in, g_out, taps, shard, wide):
+    shapes = [(taps, shard)] + [(1, shard)] * 5 + [(1, wide), g_in.shape, g_out.shape]
+    return pl.pallas_call(
+        partial(close_kernel, taps=taps),
+        out_shape=tuple(jax.ShapeDtypeStruct(s, F32) for s in shapes),
+        name="close",
+    )(small, g_in, g_out)
+
+
 def on_device(
     mel_clips,
     live_counts,
@@ -693,19 +790,20 @@
     sizes,
 ):
     shard, taps = conv_weight.shape
-    kinds = taps + 5
     hid = in_weight.shape[1]
     devices = lax.axis_size(("dp", "fsdp"))
     chans = shard * devices
     wide = in_bias.shape[0]
     lead = (sizes[0], 2, sizes[2], sizes[1])
 
-    lines = jnp.stack([conv_bias, norm_gain, norm_shift, out_bias, layer_scale])
-    lines = jnp.pad(jnp.concatenate([conv_weight.T, lines]), ((0, 0), (0, 128 - shard)))
-    last = jnp.pad(in_bias[None, :], ((0, 15 - kinds), (0, 128 - wide)))
-    small, full_in, full_out = gather_call(sizes, jnp.concatenate([lines, last]), in_weight, out_weight)
+    counts = live_counts.reshape(-1)
+    vectors = [v[None, :] for v in (conv_bias, norm_gain, norm_shift, out_bias, layer_scale)]
+    small, full_in, full_out, order = gather_call(
+        sizes, counts, mel_clips.shape[0], conv_weight.T, vectors, in_bias[None, :], in_weight, out_weight
+    )
     block_out, grad_clips, grad_in, grad_out, small = clip_call(
-        live_counts.reshape(-1),
+        counts,
+        order,
         mel_clips,
         cotangent,
         full_in.reshape(chans, hid),
@@ -719,18 +817,22 @@
         grad_in.reshape(lead + in_weight.shape),
         grad_out.reshape(lead + out_weight.shape),
     )
+    conv, cbias, gain, shift, obias, scale, ibias, grad_in, grad_out = close_call(
+        small, grad_in, grad_out, taps, shard, wide
+    )
+    vector = lambda v: v.reshape(-1)
     return (
         block_out,
         grad_clips,
-        small[:taps, :shard].T,
-        small[taps, :shard],
-        small[taps + 1, :shard],
-        small[taps + 2, :shard],
+        conv.T,
+        vector(cbias),
+        vector(gain),
+        vector(shift),
         grad_in,
-        small[kinds, :wide],
+        vector(ibias),
         grad_out,
-        small[taps + 3, :shard],
-        small[taps + 4, :shard],
+        vector(obias),
+        vector(scale),
     )
 
 

time: 160 us -> 140 us (0.88)
  Pallas kernels: 147 us -> 138 us
  local copies, waits for them, and re-layouts: 8.34 us -> 0 us
    pallas_call x2 -> x3, Pallas kernels: 63.3 us -> 56.3 us  [the longest x1 30.2 us: gather_call(): pl.pallas_call(partial(gather_kernel, sizes=sizes, cuts=cuts, slots=clips...]
    unnamed x2 -> x0, local copies, waits for them, and re-layouts: 3.08 us -> none
    squeeze x2 -> x0, local copies, waits for them, and re-layouts: 2.56 us -> none  [the longest x1 1.36 us: on_device(): small[taps + 4, :shard]]
    pallas_call x1, Pallas kernels: 83.7 us -> 81.7 us  [clip_call(): pl.pallas_call(partial(clip_kernel, taps=taps, hid_chunk=256, row_chunk=3...]
where the time goes in v1:
time: 140 us; the launch traced here: 139 us
  Pallas kernels  138 us (99%)
    pallas_call x1, Pallas kernels, clip_call(): pl.pallas_call(partial(clip_kernel, taps=taps, hid_chunk=256, row_chunk=3...  81.7 us
    pallas_call x1, Pallas kernels, gather_call(): pl.pallas_call(partial(gather_kernel, sizes=sizes, cuts=cuts, slots=clips...  30.2 us
    pallas_call x1, Pallas kernels, scatter_call(): pl.pallas_call(partial(scatter_kernel, sizes=sizes, cuts=cuts), out_shape...  24.5 us

profile of v1, /device:TPU:0, one launch (start us, length us, event | category | flops | bytes accessed | tf_op | source)
XLA Modules:
  0.0 138.7 jit_solution(1694810535034091545)
XLA Ops:
  0.6 30.2 %gather.1 = (bf16[2,2,4,2,16,128]{5,4,3,2,1,0:T(8,128)(2,1)}, bf16[2,2,4,2,16,1536]{5,4,3,2,1,0:T(8,128)(2,1)}, bf16[2,2,4,2,48,512]{5,4,3,2,1,0:T(8,128)(2,1)}, s32[20]{0:T(128)}) custom-call(s32[4]{0:T(128)} %bitcast.27, bf16[7,16]{1,0:T(8,128)(2,1)} %bitcast.29, bf16[1,16]{1,0:T(2,128)(2,1)} %bitcast.30, bf16[1,16]{1,0:T(2,128)(2,1)} %bitcast.31, ...), custom_call_target="tpu_custom_call" | custom-call | tf_op jit(solution)/shard_map/gather/pallas_call | solution.py:548
  30.8 81.7 %clips.1 = (bf16[20,256,512]{2,1,0:T(8,128)(2,1)}, bf16[20,256,512]{2,1,0:T(8,128)(2,1)}, bf16[512,1536]{1,0:T(8,128)(2,1)}, bf16[1536,512]{1,0:T(8,128)(2,1)}, f32[32,16,128]{2,1,0:T(8,128)}) custom-call(s32[4]{0:T(128)} %bitcast.28, s32[20]{0:T(128)} %get-tuple-element.32.order_ref, bf16[20,256,512]{2,1,0:T(8,128)(2,1)} %xn_ref.1, ...), custom_call_target="tpu_custom_call" | custom-call | tf_op jit(solution)/shard_map/clips/pallas_call | solution.py:309
  112.5 24.5 %scatter.1 = (f32[16,128]{1,0:T(8,128)}, f32[16,1536]{1,0:T(8,128)}, f32[48,512]{1,0:T(8,128)}) custom-call(f32[2,2,4,2,16,128]{5,4,3,2,1,0:T(8,128)} %bitcast.25, bf16[2,2,4,2,16,1536]{5,4,3,2,1,0:T(8,128)(2,1)} %bitcast.23, bf16[2,2,4,2,48,512]{5,4,3,2,1,0:T(8,128)(2,1)} %bitcast.24), custom_call_target="tpu_custom_call" | custom-call | tf_op jit(solution)/shard_map/scatter/pallas_call | solution.py:734
  137.0 1.7 %close.1 = (f32[7,16]{1,0:T(8,128)}, f32[1,16]{1,0:T(1,128)}, f32[1,16]{1,0:T(1,128)}, f32[1,16]{1,0:T(1,128)}, f32[1,16]{1,0:T(1,128)}, /*index=5*/f32[1,16]{1,...) custom-call(f32[16,128]{1,0:T(8,128)} %get-tuple-element.41.small_ref, ...), custom_call_target="tpu_custom_call" | custom-call | tf_op jit(solution)/shard_map/close/pallas_call | solution.py:769

commit v2 on v1

--- a/solution.py
+++ b/solution.py
@@ -9,6 +9,7 @@
 F32 = jnp.float32
 BF16 = jnp.bfloat16
 PAD = 8
+ONES = 16
 ROOT_HALF = 0.7071067811865476
 LOG2E = 1.4426950408889634
 INV_ROOT_2PI = 0.3989422804014327
@@ -71,15 +72,14 @@
             ib_ref[0:1, at * 128 + 128 : at * 128 + 256] += jnp.where(line < off, moved, 0.0)
 
 
-def pack_small(acc_small, acc_ib, rows_ref, small_ref):
+def pack_small(acc_small, bias, rows_ref, small_ref):
     devices = small_ref.shape[0]
     kinds = acc_small.shape[0]
     shard = rows_ref.shape[1] // devices
-    wide = acc_ib.shape[1] // devices
+    wide = bias.shape[1] // devices
     for k in range(kinds):
         rows_ref[k : k + 1, :] = jnp.sum(acc_small[k], axis=0, keepdims=True)
     lane = lane_ids(16)
-    bias = acc_ib[...]
     for d in range(devices):
         at, off = divmod(d * shard, 128)
         moved = pltpu.roll(rows_ref[:, at * 128 : at * 128 + 128], (128 - off) % 128, 1)
@@ -122,7 +122,6 @@
     raw,
     acc,
     acc_small,
-    acc_ib,
     *,
     taps,
     hid_chunk,
@@ -177,15 +176,15 @@
                 gob[to, at_rows, span[g]] = (dy_in[0, at_rows, span[g]].astype(F32) * row(scale, g)).astype(BF16)
 
     def turn(to):
-        left[to, 0] = gob[to].T
-        left[to, 1] = nb[to].T
+        left[to, 0, 0:chans] = gob[to].T
+        left[to, 1, 0:chans] = nb[to].T
 
     @pl.when(step == 0)
     def _():
         unpack_small(pieces_ref, taps + 5, rows_ref, ib_ref)
         acc[...] = jnp.zeros_like(acc)
         acc_small[...] = jnp.zeros_like(acc_small)
-        acc_ib[...] = jnp.zeros_like(acc_ib)
+        left[:, :, chans:, :] = jnp.ones((2, 2, ONES, frames), BF16)
         edge = jnp.zeros((2, groups, PAD, lanes), F32)
         xp[:, :, 0:PAD, :] = edge
         xp[:, :, PAD + frames :, :] = edge
@@ -211,9 +210,7 @@
             slope = cdf + h * (jnp.exp2(u * u * (-LOG2E)) * INV_ROOT_2PI)
             acts[0, :, cols] = (h * cdf).astype(BF16)
             ga = dot_nt(gob[now], w_out_ref[cols, :])
-            gh = (ga * slope).astype(BF16)
-            acts[1, :, cols] = gh
-            acc_ib[:, cols] += fold8(gh.astype(F32))
+            acts[1, :, cols] = (ga * slope).astype(BF16)
 
         wide = 256
         tall = frames // (2 * (chans // wide))
@@ -251,7 +248,7 @@
                 o = raw[at_rows, span[g]] + row(obias, g)
                 dy = dy_ref[0, at_rows, span[g]].astype(F32)
                 acc_small[scale, :, span[g]] += fold8(dy * o)
-                acc_small[obias, :, span[g]] += fold8(gob[now, at_rows, span[g]].astype(F32))
+                acc_small[obias, :, span[g]] += fold8(dy)
                 x = xp[now, g, pl.ds(base + PAD, rows_each), :]
                 out_ref[0, at_rows, span[g]] = (x + o * row(scale, g)).astype(BF16)
 
@@ -269,7 +266,8 @@
         def weights(unit):
             side, place = unit % 2, unit // 2
             cols = slice(place * hid_chunk, (place + 1) * hid_chunk)
-            acc[side, :, cols] += dot_nn(left[now, side], acts[side, :, cols])
+            tall = chans + ONES * side
+            acc[side, 0:tall, cols] += dot_nn(left[now, side, 0:tall], acts[side, :, cols])
 
         done = 0
         for i in range(parts):
@@ -285,10 +283,13 @@
 
     @pl.when(step == pl.num_programs(0) - 1)
     def _():
-        gin_ref[...] = acc[1].astype(gin_ref.dtype)
+        gin_ref[...] = acc[1, 0:chans].astype(gin_ref.dtype)
         for j in range(0, hid, 128):
-            gout_ref[j : j + 128, :] = acc[0, :, j : j + 128].T.astype(gout_ref.dtype)
-        pack_small(acc_small, acc_ib, rows_ref, small_ref)
+            gout_ref[j : j + 128, :] = acc[0, 0:chans, j : j + 128].T.astype(gout_ref.dtype)
+        bias = acc[1, chans : chans + 8, :] * 0.125
+        for g in range(groups):
+            acc_small[obias, :, span[g]] *= row(scale, g)
+        pack_small(acc_small, bias, rows_ref, small_ref)
 
 
 def clip_call(counts, order, x, dy, w_in, w_out, pieces, taps, grad_dtype=BF16):
@@ -341,15 +342,14 @@
                 pltpu.VMEM((groups, frames + 2 * PAD, 128), F32),
                 pltpu.VMEM((2, groups, frames, 128), F32),
                 pltpu.VMEM((2, frames, 128), F32),
-                pltpu.VMEM((2, 2, chans, frames), BF16),
+                pltpu.VMEM((2, 2, chans + ONES, frames), BF16),
                 pltpu.VMEM((2, frames, hid), BF16),
                 pltpu.VMEM((2, frames, chans), BF16),
                 pltpu.VMEM((2, frames, chans), BF16),
                 pltpu.VMEM((frames, chans), F32),
                 pltpu.VMEM((frames, chans), F32),
-                pltpu.VMEM((2, chans, hid), F32),
+                pltpu.VMEM((2, chans + ONES, hid), F32),
                 pltpu.VMEM((kinds, 8, chans), F32),
-                pltpu.VMEM((8, hid), F32),
             ],
         ),
         compiler_params=pltpu.CompilerParams(vmem_limit_bytes=60 << 20),

time: 140 us -> 144 us (1.029)
  Pallas kernels: 138 us -> 143 us
    pallas_call x1, Pallas kernels: 24.5 us -> 51.1 us  [scatter_call(): pl.pallas_call(partial(scatter_kernel, sizes=sizes, cuts=cuts), out_shape...]
    pallas_call x1, Pallas kernels: 81.7 us -> 59.7 us  [clip_call(): pl.pallas_call(partial(clip_kernel, taps=taps, hid_chunk=256, row_chunk=3...]
where the time goes in v2:
time: 144 us; the launch traced here: 143 us
  Pallas kernels  143 us (99%)
    pallas_call x1, Pallas kernels, clip_call(): pl.pallas_call(partial(clip_kernel, taps=taps, hid_chunk=256, row_chunk=3...  59.7 us
    pallas_call x1, Pallas kernels, scatter_call(): pl.pallas_call(partial(scatter_kernel, sizes=sizes, cuts=cuts), out_shape...  51.1 us
    pallas_call x1, Pallas kernels, gather_call(): pl.pallas_call(partial(gather_kernel, sizes=sizes, cuts=cuts, slots=clips...  30.2 us

profile of v2, /device:TPU:0, one launch (start us, length us, event | category | flops | bytes accessed | tf_op | source)
XLA Modules:
  0.0 143.4 jit_solution(10043223836740751683)
XLA Ops:
  0.6 30.2 %gather.1 = (bf16[2,2,4,2,16,128]{5,4,3,2,1,0:T(8,128)(2,1)}, bf16[2,2,4,2,16,1536]{5,4,3,2,1,0:T(8,128)(2,1)}, bf16[2,2,4,2,48,512]{5,4,3,2,1,0:T(8,128)(2,1)}, s32[20]{0:T(128)}) custom-call(s32[4]{0:T(128)} %bitcast.27, bf16[7,16]{1,0:T(8,128)(2,1)} %bitcast.29, bf16[1,16]{1,0:T(2,128)(2,1)} %bitcast.30, bf16[1,16]{1,0:T(2,128)(2,1)} %bitcast.31, ...), custom_call_target="tpu_custom_call" | custom-call | tf_op jit(solution)/shard_map/gather/pallas_call | solution.py:548
  30.8 59.7 %clips.1 = (bf16[20,256,512]{2,1,0:T(8,128)(2,1)}, bf16[20,256,512]{2,1,0:T(8,128)(2,1)}, bf16[512,1536]{1,0:T(8,128)(2,1)}, bf16[1536,512]{1,0:T(8,128)(2,1)}, f32[32,16,128]{2,1,0:T(8,128)}) custom-call(s32[4]{0:T(128)} %bitcast.28, s32[20]{0:T(128)} %get-tuple-element.32.order_ref, bf16[20,256,512]{2,1,0:T(8,128)(2,1)} %xn_ref.1, ...), custom_call_target="tpu_custom_call" | custom-call | tf_op jit(solution)/shard_map/clips/pallas_call | solution.py:310
  90.6 51.1 %scatter.1 = (f32[16,128]{1,0:T(8,128)}, f32[16,1536]{1,0:T(8,128)}, f32[48,512]{1,0:T(8,128)}) custom-call(f32[2,2,4,2,16,128]{5,4,3,2,1,0:T(8,128)} %bitcast.25, bf16[2,2,4,2,16,1536]{5,4,3,2,1,0:T(8,128)(2,1)} %bitcast.23, bf16[2,2,4,2,48,512]{5,4,3,2,1,0:T(8,128)(2,1)} %bitcast.24), custom_call_target="tpu_custom_call" | custom-call | tf_op jit(solution)/shard_map/scatter/pallas_call | solution.py:734
  141.7 1.7 %close.1 = (f32[7,16]{1,0:T(8,128)}, f32[1,16]{1,0:T(1,128)}, f32[1,16]{1,0:T(1,128)}, f32[1,16]{1,0:T(1,128)}, f32[1,16]{1,0:T(1,128)}, /*index=5*/f32[1,16]{1,...) custom-call(f32[16,128]{1,0:T(8,128)} %get-tuple-element.41.small_ref, ...), custom_call_target="tpu_custom_call" | custom-call | tf_op jit(solution)/shard_map/close/pallas_call | solution.py:769
